TPU v7x, 32 devices: a whole 2x2x4 slice. The times are simulated.
32 devices in a mesh: row: 2 (over y), col: 4 (over z), rep: 4 (over x, core).
Axes of the slice: x: 2, y: 2, z: 4, core: 2. Of those that a mesh axis runs over, the one named last changes fastest.
Arguments:
- amplitudes: float32 [18432, 18432], P('row', ('col', 'rep')), may hold values from -0.046875 to 0.046875
- cycle_ints: float32 [18432, 288], P(('col', 'rep'), 'row'), may hold values from -6 to 6
Outputs:
- cycle_term: float32 [18432, 288], P(('row', 'rep'), 'col')
All inputs are finite; a program needn't handle non-finite values.
Results may differ from a plain program's by a relative error of at most 0.0002.
Values sent between devices are 32-bit elements; how exact they have to be, the bound alone decides.
No kernel may reach another device: no remote copies, remote signals or barrier semaphores. Data moves between devices by JAX's collectives and lax.ppermute only.
A program may use at most 128 MiB of HBM per device.

v0:
```python
import jax
import jax.numpy as jnp
from jax import lax
from jax.sharding import PartitionSpec as P


def passed_along(x, axis, by):
    devices = lax.axis_size(axis)
    return lax.ppermute(x, axis, [(i, (i + by) % devices) for i in range(devices)])


def per_device(amplitudes, cycle_ints):
    n_col = lax.axis_size("col")
    full_ints = lax.all_gather(cycle_ints, "row", axis=1, tiled=True)
    width = full_ints.shape[1] // n_col
    here = lax.axis_index("col")
    n_rows = amplitudes.shape[0]

    def product(block, offset, count):
        columns = lax.dynamic_slice_in_dim(full_ints, block * width + offset, count, 1)
        return jnp.dot(
            amplitudes, columns, precision=lax.Precision.HIGHEST, preferred_element_type=jnp.float32
        )

    def advance(step, partial_sum):
        block = (here - step) % n_col
        partial_sum = partial_sum + product(block, 0, width)
        return passed_along(partial_sum, "col", 1)

    totals = lax.fori_loop(0, n_col, advance, jnp.zeros((n_rows, width), jnp.float32))
    return lax.psum_scatter(totals, "rep", scatter_dimension=0, tiled=True)


def solution(mesh):
    return jax.shard_map(
        per_device,
        mesh=mesh,
        in_specs=(P("row", ("col", "rep")), P(("col", "rep"), "row")),
        out_specs=P(("row", "rep"), "col"),
        check_vma=False,
    )
```

profile of v0, /device:TPU:0, one launch (start us, length us, event | category | flops | bytes accessed | tf_op | source)
XLA Modules:
  0.0 501.8 jit_solution(8955206366546756683)
XLA Ops:
  6.5 0.0 all-gather.2.cloned.1.call-start
  6.5 0.7 all-gather.2.cloned.1.call-update
  7.3 0.0 reduce-scatter.2.cloned.1.call-start
  7.3 28.7 %all-gather.2.cloned.1.call-done = f32[1152,288]{0,1:T(8,128)} async-done(((f32[1152,144]{0,1:T(8,128)}), f32[1152,288]{0,1:T(8,128)}) %all-gather.2.cloned.1.call-update) | async-done | bytes 1327120 | tf_op jit(solution)/shard_map/all_gather | solution.py:14
  36.0 0.2 broadcast_in_dim.3
  36.3 425.1 %while.15 = (s32[]{:T(128)}, f32[9216,72]{0,1:T(8,128)S(1)}, s32[]{:T(128)}, f32[1152,288]{0,1:T(8,128)}, f32[9216,1152]{1,0:T(8,128)}, /*index=5*/s32[]{:T(128)...) while((s32[]{:T(128)}, f32[9216,72]{0,1:T(8,128)S(1)}, s32[]{:T(128)}, ...), condition=%wide.region_1.2_spmd, body=%wide.region_0.1_spmd.sunk | while | flops 9173606400 | bytes 58724672 | solution.py:30
  36.3 46.4 %fusion.9 = f32[9216,72]{0,1:T(8,128)} fusion(f32[9216,72]{0,1:T(8,128)S(1)} %get-tuple-element.197, f32[9216,1152]{1,0:T(8,128)} %get-tuple-element.211, f32[1152,288]{0,1:T(8,128)} %get-tuple-element.210, s32[]{:T(128)S(6)} %select_n.33), kind=kOutput, calls=%fused_computation.1.clone.1 | convolution fusion | flops 9173606400 | bytes 48107524 | tf_op jit(solution)/shard_map/while/body/eval_jaxpr/dot_general | solution.py:21
  82.7 1.5 collective-permute-start
  84.2 59.7 %collective-permute-done = f32[9216,72]{0,1:T(8,128)S(1)} collective-permute-done((f32[9216,72]{0,1:T(8,128)}, f32[9216,72]{0,1:T(8,128)S(1)}, u32[]{:S(2)}, u32[]{:S(2)}) %collective-permute-start) | collective-permute-done | bytes 2654240 | tf_op jit(solution)/shard_map/while/body/eval_jaxpr/ppermute | solution.py:9
  143.9 46.4 %fusion.9 = f32[9216,72]{0,1:T(8,128)} fusion(f32[9216,72]{0,1:T(8,128)S(1)} %get-tuple-element.197, f32[9216,1152]{1,0:T(8,128)} %get-tuple-element.211, f32[1152,288]{0,1:T(8,128)} %get-tuple-element.210, s32[]{:T(128)S(6)} %select_n.33), kind=kOutput, calls=%fused_computation.1.clone.1 | convolution fusion | flops 9173606400 | bytes 48107524 | tf_op jit(solution)/shard_map/while/body/eval_jaxpr/dot_general | solution.py:21
  190.3 0.0 collective-permute-start
  190.3 60.3 %collective-permute-done = f32[9216,72]{0,1:T(8,128)S(1)} collective-permute-done((f32[9216,72]{0,1:T(8,128)}, f32[9216,72]{0,1:T(8,128)S(1)}, u32[]{:S(2)}, u32[]{:S(2)}) %collective-permute-start) | collective-permute-done | bytes 2654240 | tf_op jit(solution)/shard_map/while/body/eval_jaxpr/ppermute | solution.py:9
  250.6 46.4 %fusion.9 = f32[9216,72]{0,1:T(8,128)} fusion(f32[9216,72]{0,1:T(8,128)S(1)} %get-tuple-element.197, f32[9216,1152]{1,0:T(8,128)} %get-tuple-element.211, f32[1152,288]{0,1:T(8,128)} %get-tuple-element.210, s32[]{:T(128)S(6)} %select_n.33), kind=kOutput, calls=%fused_computation.1.clone.1 | convolution fusion | flops 9173606400 | bytes 48107524 | tf_op jit(solution)/shard_map/while/body/eval_jaxpr/dot_general | solution.py:21
  297.0 0.0 collective-permute-start
  297.0 59.4 %collective-permute-done = f32[9216,72]{0,1:T(8,128)S(1)} collective-permute-done((f32[9216,72]{0,1:T(8,128)}, f32[9216,72]{0,1:T(8,128)S(1)}, u32[]{:S(2)}, u32[]{:S(2)}) %collective-permute-start) | collective-permute-done | bytes 2654240 | tf_op jit(solution)/shard_map/while/body/eval_jaxpr/ppermute | solution.py:9
  356.4 46.4 %fusion.9 = f32[9216,72]{0,1:T(8,128)} fusion(f32[9216,72]{0,1:T(8,128)S(1)} %get-tuple-element.197, f32[9216,1152]{1,0:T(8,128)} %get-tuple-element.211, f32[1152,288]{0,1:T(8,128)} %get-tuple-element.210, s32[]{:T(128)S(6)} %select_n.33), kind=kOutput, calls=%fused_computation.1.clone.1 | convolution fusion | flops 9173606400 | bytes 48107524 | tf_op jit(solution)/shard_map/while/body/eval_jaxpr/dot_general | solution.py:21
  402.8 0.0 collective-permute-start
  402.8 58.6 %collective-permute-done = f32[9216,72]{0,1:T(8,128)S(1)} collective-permute-done((f32[9216,72]{0,1:T(8,128)}, f32[9216,72]{0,1:T(8,128)S(1)}, u32[]{:S(2)}, u32[]{:S(2)}) %collective-permute-start) | collective-permute-done | bytes 2654240 | tf_op jit(solution)/shard_map/while/body/eval_jaxpr/ppermute | solution.py:9
  461.4 0.0 copy-start
  461.4 1.5 copy-done
  462.9 0.0 reduce-scatter.2.cloned.1.call-update
  462.9 32.0 %reduce-scatter.2.cloned.1.call-done = f32[2304,72]{0,1:T(8,128)} async-done(((f32[9216,72]{0,1:T(8,128)}), f32[2304,72]{0,1:T(8,128)}) %reduce-scatter.2.cloned.1.call-update) | async-done | bytes 663568 | tf_op jit(solution)/shard_map/reduce_scatter | solution.py:31
Async XLA Ops:
  6.5 29.5 %all-gather.2.cloned.1.call-start = ((), (), s32[]{:S(2)}) async-start(), calls=%async_computation.1 | async-start | bytes 1990656 | tf_op jit(solution)/shard_map/all_gather | solution.py:14
  7.3 487.7 %reduce-scatter.2.cloned.1.call-start = ((), (), s32[]{:S(2)}) async-start(), calls=%async_computation.2 | async-start | bytes 3317760 | tf_op jit(solution)/shard_map/reduce_scatter | solution.py:31
  82.7 61.1 %collective-permute-start = (f32[9216,72]{0,1:T(8,128)}, f32[9216,72]{0,1:T(8,128)S(1)}, u32[]{:S(2)}, u32[]{:S(2)}) collective-permute-start(f32[9216,72]{0,1:T(8,128)} %fusion.9), channel_id=1, source_target_pairs={{0,4},{4,8},{8,12},{12,0},{1,5},{5,9},{9,13},{13,1},{2,6},{6,10},{... | collective-permute-start | bytes 7962632 | tf_op jit(solution)/shard_map/while/body/eval_jaxpr/ppermute | solution.py:9
  190.3 60.3 %collective-permute-start = (f32[9216,72]{0,1:T(8,128)}, f32[9216,72]{0,1:T(8,128)S(1)}, u32[]{:S(2)}, u32[]{:S(2)}) collective-permute-start(f32[9216,72]{0,1:T(8,128)} %fusion.9), channel_id=1, source_target_pairs={{0,4},{4,8},{8,12},{12,0},{1,5},{5,9},{9,13},{13,1},{2,6},{6,10},{... | collective-permute-start | bytes 7962632 | tf_op jit(solution)/shard_map/while/body/eval_jaxpr/ppermute | solution.py:9
  297.0 59.4 %collective-permute-start = (f32[9216,72]{0,1:T(8,128)}, f32[9216,72]{0,1:T(8,128)S(1)}, u32[]{:S(2)}, u32[]{:S(2)}) collective-permute-start(f32[9216,72]{0,1:T(8,128)} %fusion.9), channel_id=1, source_target_pairs={{0,4},{4,8},{8,12},{12,0},{1,5},{5,9},{9,13},{13,1},{2,6},{6,10},{... | collective-permute-start | bytes 7962632 | tf_op jit(solution)/shard_map/while/body/eval_jaxpr/ppermute | solution.py:9
  402.8 58.6 %collective-permute-start = (f32[9216,72]{0,1:T(8,128)}, f32[9216,72]{0,1:T(8,128)S(1)}, u32[]{:S(2)}, u32[]{:S(2)}) collective-permute-start(f32[9216,72]{0,1:T(8,128)} %fusion.9), channel_id=1, source_target_pairs={{0,4},{4,8},{8,12},{12,0},{1,5},{5,9},{9,13},{13,1},{2,6},{6,10},{... | collective-permute-start | bytes 7962632 | tf_op jit(solution)/shard_map/while/body/eval_jaxpr/ppermute | solution.py:9
  461.4 1.5 copy-start
Sparse Core Ops, SparseCore 0:
  8.9 27.1 all-gather.1
  463.0 31.8 reduce-scatter.1
where the time goes:
time: 502 us
  waiting for transfers between devices  299 us (60%)
  matrix products  186 us (37%)
  between operations  13.4 us (3%)
    ppermute x4, waiting for transfers between devices, passed_along(): lax.ppermute(x, axis, [(i, (i + by) % devices) for i in range(devices)])  238 us
    dot_general x4, matrix products, product(): jnp.dot(amplitudes, columns, precision=lax.Precision.HIGHEST, preferred_e...  186 us
    reduce_scatter x1, waiting for transfers between devices, per_device(): return lax.psum_scatter(totals, 'rep', scatter_dimension=0, tiled=True)  32 us
    all_gather x1, waiting for transfers between devices, per_device(): full_ints = lax.all_gather(cycle_ints, 'row', axis=1, tiled=True)  28.7 us
  transfers between devices with their start and end apart: 6, of which 6 were waited for; matrix products, arithmetic and copies ran while one was open for 0% of the time, Pallas kernels for 0%

commit v1 on v0

v1 whole, which is shorter than its diff:
```python
import functools
import math
import re

import jax
import jax.numpy as jnp
from jax import lax
from jax.experimental import pallas as pl
from jax.experimental.pallas import tpu as pltpu
from jax.sharding import PartitionSpec as P


LANES = 128
SLOTS = 3
PAIR = 2
PIECES = (4, 4, 4, 2, 2, 2)
ORDER = (
    "S0a", "T0a", "S0b", "S1ab", "T0b", "T1S2ab", "Z0a", "Z0b", "T2S3ab", "F0", "T3S4ab", "Z1ab", "T4S5ab",
    "Z2ab", "F1", "T5ab", "Z3ab", "F2", "Z4ab", "F3", "Z5ab", "F4", "F5",
)
EVENT = re.compile(r"(?:T(\d))?(?:S(\d))?(?:([ZF])(\d))?([ab]*)$")
CONTRACT_LAST = (((1,), (1,)), ((), ()))
VMEM = pl.BlockSpec(memory_space=pltpu.VMEM)


def halves(x):
    high = x.astype(jnp.bfloat16)
    return high, (x - high.astype(jnp.float32)).astype(jnp.bfloat16)


def products(place, amplitudes, ints, close, beside):
    depth = amplitudes.shape[1]
    n_cols = sum(part.shape[0] for part in ints)
    block_rows = amplitudes.shape[0] // 4 // LANES
    size = PAIR * LANES
    n_close = close[1] // PAIR if close else 0
    n_beside = beside[1] // PAIR if beside else 0
    tiles = n_close + n_beside
    slots = min(SLOTS, tiles)
    args = [amplitudes, *ints]
    out_shape = []
    if close:
        args.append(close[2])
        out_shape += [jax.ShapeDtypeStruct((1, n_cols, close[1] * LANES), jnp.float32)] * 2
    if beside:
        out_shape.append(jax.ShapeDtypeStruct((2, n_cols, beside[1] * LANES), jnp.float32))

    def kernel(place_ref, rows_ref, *refs):
        *refs, high_ref, low_ref, held, arrived = refs
        ints_refs, rest = refs[: len(ints)], refs[len(ints):]

        def fetch(tile, half):
            chip, core = place_ref[2] >> 1, place_ref[2] & 1
            if tile < n_close:
                block = 2 * (chip if half else 1 - chip) + core
                at = close[0] + tile * PAIR
            else:
                block = 2 * half + 1 - core
                at = beside[0] + (tile - n_close) * PAIR
            first = pl.multiple_of((block * block_rows + at) * LANES, LANES)
            slot = tile % slots
            return pltpu.make_async_copy(
                rows_ref.at[pl.ds(first, size), :],
                held.at[slot, pl.ds(half * size, size), :],
                arrived.at[slot, half],
            )

        for tile in range(slots):
            for half in range(2):
                fetch(tile, half).start()
        at = 0
        for ref in ints_refs:
            to = pl.ds(at, ref.shape[0])
            high_ref[to, :], low_ref[to, :] = halves(ref[...])
            at += ref.shape[0]
        dot = functools.partial(
            lax.dot_general, dimension_numbers=CONTRACT_LAST, preferred_element_type=jnp.float32
        )
        for tile in range(tiles):
            for half in range(2):
                fetch(tile, half).wait()
            a_high, a_low = halves(held[tile % slots])
            result = dot(high_ref[...], a_high) + (
                dot(low_ref[...], a_high) + dot(high_ref[...], a_low)
            )
            if tile < n_close:
                came_ref, far_ref, near_ref = rest[:3]
                chip_here = place_ref[2] >> 1
                lanes = pl.ds(tile * size, size)
                far_ref[0, :, lanes] = result[:, :size] + came_ref[1 - chip_here, :, lanes]
                near_ref[0, :, lanes] = result[:, size:] + came_ref[chip_here, :, lanes]
            else:
                lanes = pl.ds((tile - n_close) * size, size)
                rest[-1][0, :, lanes] = result[:, :size]
                rest[-1][1, :, lanes] = result[:, size:]
            if tile + slots < tiles:
                for half in range(2):
                    fetch(tile + slots, half).start()

    rows = 2 * tiles * size
    return pl.pallas_call(
        kernel,
        out_shape=out_shape,
        grid_spec=pltpu.PrefetchScalarGridSpec(
            num_scalar_prefetch=1,
            grid=(),
            in_specs=[pl.BlockSpec(memory_space=pl.ANY)] + [VMEM] * (len(args) - 1),
            out_specs=[VMEM] * len(out_shape),
            scratch_shapes=[pltpu.VMEM((n_cols, depth), jnp.bfloat16)] * 2
            + [
                pltpu.VMEM((slots, 2 * size, depth), jnp.float32),
                pltpu.SemaphoreType.DMA((slots, 2)),
            ],
        ),
        compiler_params=pltpu.CompilerParams(vmem_limit_bytes=17 << 20),
        cost_estimate=pl.CostEstimate(
            flops=6 * rows * n_cols * depth, bytes_accessed=4 * rows * depth, transcendentals=0
        ),
        name="products",
    )(place, *args)


def small(kernel, shapes, place, args):
    size = 4 * sum(math.prod(shape) for shape in shapes) + sum(4 * x.size for x in args)
    return pl.pallas_call(
        kernel,
        out_shape=[jax.ShapeDtypeStruct(shape, jnp.float32) for shape in shapes],
        grid_spec=pltpu.PrefetchScalarGridSpec(
            num_scalar_prefetch=1,
            grid=(),
            in_specs=[VMEM] * len(args),
            out_specs=[VMEM] * len(shapes),
        ),
        compiler_params=pltpu.CompilerParams(vmem_limit_bytes=8 << 20),
        cost_estimate=pl.CostEstimate(flops=size, bytes_accessed=size, transcendentals=0),
        name="sums",
    )(place, *args)


def z_kernel(place_ref, near_ref, far_ref, sent_ref, keeps_ref):
    bit = place_ref[1] & 1
    for part in range(near_ref.shape[0]):
        sent_ref[part] = near_ref[part, 1 - bit] + far_ref[part, 1 - bit]
        keeps_ref[part] = near_ref[part, bit] + far_ref[part, bit]


def f_kernel(place_ref, *refs):
    *sums, sent_ref, stays_ref = refs
    half = (place_ref[1] >> 1) ^ place_ref[0]
    if len(sums) == 2:
        keeps_ref, came_ref = sums
        sent_ref[...] = keeps_ref[1 - half] + came_ref[1 - half]
        stays_ref[...] = keeps_ref[half] + came_ref[half]
        return
    own = sums[0][0] + sums[1][0]
    other = sums[2][0] + sums[3][0]
    sent_ref[...] = jnp.where(half == 0, other, own)
    stays_ref[...] = jnp.where(half == 0, own, other)


def end_kernel(_, *refs):
    at = 0
    for stays_ref, came_ref in zip(refs[:-1:2], refs[1:-1:2]):
        to = pl.ds(at, stays_ref.shape[1])
        refs[-1][:, to] = stays_ref[...] + came_ref[...]
        at += stays_ref.shape[1]


def pipelined(amplitudes, cycle_ints):
    place = jnp.stack([lax.axis_index(axis) for axis in ("row", "col", "rep")]).astype(jnp.int32)
    flip = {bit: [(i, i ^ bit) for i in range(4)] for bit in (1, 2)}

    own = cycle_ints.T
    other = lax.ppermute(own, "row", [(0, 1), (1, 0)])
    sets = {"a": (own,), "b": (other,), "ab": (own, other)}
    width = own.shape[0] // 2
    scale = amplitudes.shape[0] // 4 // LANES // sum(PIECES)
    starts = [sum(PIECES[:i]) * scale for i in range(len(PIECES))]
    units = [piece * scale for piece in PIECES]

    got, far, near, kept, outs = {}, {}, {}, {}, {}
    for event in ORDER:
        close, beside, kind, piece, part = EVENT.match(event).groups()
        shape = (len(part), 2, width, -1)
        if close or beside:
            c, b = close and int(close), beside and int(beside)
            made = products(
                place,
                amplitudes,
                sets[part],
                (starts[c], units[c], got[c, part]) if close else None,
                (starts[b], units[b]) if beside else None,
            )
            if close:
                far[c, part] = lax.ppermute(made[0], "rep", flip[2]).reshape(shape)
                near[c, part] = made[1].reshape(shape)
            if beside:
                got[b, part] = lax.ppermute(made[-1], "rep", flip[1])
            continue
        piece = int(piece)
        key = (piece, part)
        if kind == "Z":
            sent, keeps = small(z_kernel, [(len(part), width, units[piece] * LANES)] * 2, place, [near[key], far[key]])
            kept[key] = keeps, lax.ppermute(sent, "col", flip[1])
        elif kind == "F":
            sums = [x for k in kept if k[0] == piece for x in kept[k]]
            sent, stays = small(f_kernel, [(width, units[piece] * LANES)] * 2, place, sums)
            outs[piece] = stays, lax.ppermute(sent, "col", flip[2])
    pairs = [x for p in range(len(PIECES)) for x in outs[p]]
    return small(end_kernel, [(width, sum(units) * LANES)], place, pairs)[0].T


def passed_along(x, axis, by):
    devices = lax.axis_size(axis)
    return lax.ppermute(x, axis, [(i, (i + by) % devices) for i in range(devices)])


def general(amplitudes, cycle_ints):
    n_col = lax.axis_size("col")
    full_ints = lax.all_gather(cycle_ints, "row", axis=1, tiled=True)
    width = full_ints.shape[1] // n_col
    here = lax.axis_index("col")
    n_rows = amplitudes.shape[0]

    def advance(step, partial_sum):
        block = (here - step) % n_col
        columns = lax.dynamic_slice_in_dim(full_ints, block * width, width, 1)
        partial_sum = partial_sum + jnp.dot(
            amplitudes, columns, precision=lax.Precision.HIGHEST, preferred_element_type=jnp.float32
        )
        return passed_along(partial_sum, "col", 1)

    totals = lax.fori_loop(0, n_col, advance, jnp.zeros((n_rows, width), jnp.float32))
    return lax.psum_scatter(totals, "rep", scatter_dimension=0, tiled=True)


def tall_enough(amplitudes, cycle_ints):
    rows, depth = amplitudes.shape
    return rows % (4 * LANES * sum(PIECES)) == 0 and depth % LANES == 0 and cycle_ints.shape[1] % 16 == 0


def solution(mesh):
    sizes = tuple(mesh.shape[axis] for axis in ("row", "col", "rep"))

    def per_device(amplitudes, cycle_ints):
        if sizes == (2, 4, 4) and tall_enough(amplitudes, cycle_ints):
            return pipelined(amplitudes, cycle_ints)
        return general(amplitudes, cycle_ints)

    return jax.shard_map(
        per_device,
        mesh=mesh,
        in_specs=(P("row", ("col", "rep")), P(("col", "rep"), "row")),
        out_specs=P(("row", "rep"), "col"),
        check_vma=False,
    )
```

time: 502 us -> 168 us (0.33)
  waiting for transfers between devices: 299 us -> 72.6 us
  matrix products: 186 us -> 0 us
  Pallas kernels: 0 us -> 60.5 us
  starting transfers between devices: 1.53 us -> 33 us
  between operations: 13.4 us -> 0.25 us
    dot_general x4 -> x0, matrix products: 186 us -> none  [product(): jnp.dot(amplitudes, columns, precision=lax.Precision.HIGHEST, preferred_e...]
    ppermute x4 -> x28, waiting for transfers between devices: 238 us -> 72.6 us  [the longest x7 30.7 us: pipelined(): far[c, part] = lax.ppermute(made[0], 'rep', flip[2]).reshape(shape)]
    pallas_call x0 -> x24, Pallas kernels: none -> 60.5 us  [the longest x10 51.5 us: products(): pl.pallas_call(kernel, out_shape=out_shape, grid_spec=pltpu.PrefetchScala...]
    reduce_scatter x1 -> x0, waiting for transfers between devices: 32 us -> none  [per_device(): return lax.psum_scatter(totals, 'rep', scatter_dimension=0, tiled=True)]
    ppermute x4 -> x28, starting transfers between devices: 1.49 us -> 33 us  [the longest x7 11.1 us: pipelined(): kept[key] = (keeps, lax.ppermute(sent, 'col', flip[1]))]
    all_gather x1 -> x0, waiting for transfers between devices: 28.7 us -> none  [per_device(): full_ints = lax.all_gather(cycle_ints, 'row', axis=1, tiled=True)]
  transfers between devices with their start and end apart: 6 -> 28, of which waited for: 6 -> 16; matrix products, arithmetic and copies ran while one was open for 0% -> 0% of each run, Pallas kernels for 0% -> 21%
where the time goes in v1:
time: 168 us; the launch traced here: 167 us
  waiting for transfers between devices  72.6 us (43%)
  Pallas kernels  60.5 us (36%)
  starting transfers between devices  33 us (20%)
    pallas_call x10, Pallas kernels, products(): pl.pallas_call(kernel, out_shape=out_shape, grid_spec=pltpu.PrefetchScala...  51.5 us
    ppermute x7, waiting for transfers between devices, pipelined(): far[c, part] = lax.ppermute(made[0], 'rep', flip[2]).reshape(shape)  30.7 us
    ppermute x6, waiting for transfers between devices, pipelined(): outs[piece] = (stays, lax.ppermute(sent, 'col', flip[2]))  18.4 us
    ppermute x1, waiting for transfers between devices, pipelined(): other = lax.ppermute(own, 'row', [(0, 1), (1, 0)])  15 us
    ppermute x7, starting transfers between devices, pipelined(): kept[key] = (keeps, lax.ppermute(sent, 'col', flip[1]))  11.1 us
    ppermute x6, starting transfers between devices, pipelined(): outs[piece] = (stays, lax.ppermute(sent, 'col', flip[2]))  9.1 us
    pallas_call x14, Pallas kernels, small(): pl.pallas_call(kernel, out_shape=[jax.ShapeDtypeStruct(shape, jnp.float32...  8.98 us
    ppermute x7, starting transfers between devices, pipelined(): far[c, part] = lax.ppermute(made[0], 'rep', flip[2]).reshape(shape)  7.98 us
  transfers between devices with their start and end apart: 28, of which 16 were waited for; matrix products, arithmetic and copies ran while one was open for 0% of the time, Pallas kernels for 21%

profile of v1, /device:TPU:0, one launch (start us, length us, event | category | flops | bytes accessed | tf_op | source)
XLA Modules:
  0.0 167.5 jit_solution(14629969404972904551)
XLA Ops:
  0.0 3.0 %collective-permute-start.3 = (f32[144,1152]{1,0:T(8,128)}, f32[144,1152]{1,0:T(8,128)S(1)}, u32[]{:S(2)}, u32[]{:S(2)}) collective-permute-start(f32[144,1152]{1,0:T(8,128)} %bitcast.19), channel_id=1, source_target_pairs={{0,16},{16,0},{1,17},{17,1},{2,18},{18,2},{3,19},{19,3},{4,20},{20... | collective-permute-start | bytes 1990664 | tf_op jit(solution)/shard_map/ppermute | solution.py:174
  3.1 15.0 %collective-permute-done.3.refs_0_.refs_1_ = f32[144,1152]{1,0:T(8,128)S(1)} collective-permute-done((f32[144,1152]{1,0:T(8,128)}, f32[144,1152]{1,0:T(8,128)S(1)}, u32[]{:S(2)}, u32[]{:S(2)}) %collective-permute-start.3) | collective-permute-done | bytes 663584 | tf_op jit(solution)/shard_map/ppermute | solution.py:174
  19.2 4.9 %products.14 = f32[2,288,512]{2,1,0:T(8,128)S(1)} custom-call(s32[3]{0:T(128)S(1)} %pad_add_fusion.place_ref._, f32[9216,1152]{1,0:T(8,128)} %rows_ref.19, f32[144,1152]{1,0:T(8,128)S(1)} %bitcast.20, f32[144,1152]{1,0:T(8,128)S(1)} %collective-permute-done.3.refs_0_.refs_1_), custom_call_target="tpu_custom_call" | custom-call | flops 2038431744 | bytes 4718592 | tf_op jit(solution)/shard_map/products/pallas_call | solution.py:101
  24.2 2.8 %collective-permute-done.8.refs_2_ = f32[2,288,512]{2,1,0:T(8,128)S(1)} collective-permute-done((f32[2,288,512]{2,1,0:T(8,128)S(1)}, f32[2,288,512]{2,1,0:T(8,128)S(1)}, u32[]{:S(2)}, u32[]{:S(2)}) %collective-permute-start.8) | collective-permute-done | bytes 1179680 | tf_op jit(solution)/shard_map/ppermute | solution.py:198
  27.0 7.6 %products.15 = (f32[1,288,512]{2,1,0:T(8,128)S(1)}, f32[1,288,512]{2,1,0:T(8,128)S(1)}, f32[2,288,512]{2,1,0:T(8,128)S(1)}) custom-call(s32[3]{0:T(128)S(1)} %pad_add_fusion.place_ref._, f32[9216,1152]{1,0:T(8,128)} %rows_ref.19, f32[144,1152]{1,0:T(8,128)S(1)} %bitcast.21, f32[144,1152]{1,0:T(8,128)S(1)} %collective-permute-done.3.refs_0_.refs_1_, ...), custom_call_target="tpu_custom_call" | custom-call | flops 4076863488 | bytes 9437184 | tf_op jit(solution)/shard_map/products/pallas_call | solution.py:101
  34.9 2.7 %collective-permute-done.12.refs_2_ = f32[2,288,512]{2,1,0:T(8,128)S(1)} collective-permute-done((f32[2,288,512]{2,1,0:T(8,128)S(1)}, f32[2,288,512]{2,1,0:T(8,128)S(1)}, u32[]{:S(2)}, u32[]{:S(2)}) %collective-permute-start.12) | collective-permute-done | bytes 1179680 | tf_op jit(solution)/shard_map/ppermute | solution.py:198
  37.6 6.3 %products.16 = (f32[1,288,512]{2,1,0:T(8,128)S(1)}, f32[1,288,512]{2,1,0:T(8,128)S(1)}, f32[2,288,256]{2,1,0:T(8,128)S(1)}) custom-call(s32[3]{0:T(128)S(1)} %pad_add_fusion.place_ref._, f32[9216,1152]{1,0:T(8,128)} %rows_ref.19, f32[144,1152]{1,0:T(8,128)S(1)} %bitcast.22, f32[144,1152]{1,0:T(8,128)S(1)} %collective-permute-done.3.refs_0_.refs_1_, ...), custom_call_target="tpu_custom_call" | custom-call | flops 3057647616 | bytes 7077888 | tf_op jit(solution)/shard_map/products/pallas_call | solution.py:101
  44.1 1.9 %collective-permute-done.16.refs_2_ = f32[2,288,256]{2,1,0:T(8,128)S(1)} collective-permute-done((f32[2,288,256]{2,1,0:T(8,128)S(1)}, f32[2,288,256]{2,1,0:T(8,128)S(1)}, u32[]{:S(2)}, u32[]{:S(2)}) %collective-permute-start.16) | collective-permute-done | bytes 589856 | tf_op jit(solution)/shard_map/ppermute | solution.py:198
  46.0 4.9 %products.17 = (f32[1,288,256]{2,1,0:T(8,128)S(1)}, f32[1,288,256]{2,1,0:T(8,128)S(1)}, f32[2,288,256]{2,1,0:T(8,128)S(1)}) custom-call(s32[3]{0:T(128)S(1)} %pad_add_fusion.place_ref._, f32[9216,1152]{1,0:T(8,128)} %rows_ref.19, f32[144,1152]{1,0:T(8,128)S(1)} %bitcast.23, f32[144,1152]{1,0:T(8,128)S(1)} %collective-permute-done.3.refs_0_.refs_1_, ...), custom_call_target="tpu_custom_call" | custom-call | flops 2038431744 | bytes 4718592 | tf_op jit(solution)/shard_map/products/pallas_call | solution.py:101
  51.1 5.0 %products.10 = f32[2,144,512]{2,1,0:T(8,128)S(1)} custom-call(s32[3]{0:T(128)S(1)} %pad_add_fusion.place_ref._, f32[9216,1152]{1,0:T(8,128)} %rows_ref.19, f32[144,1152]{1,0:T(8,128)S(1)} %bitcast.24), custom_call_target="tpu_custom_call" | custom-call | flops 1019215872 | bytes 4718592 | tf_op jit(solution)/shard_map/products/pallas_call | solution.py:101
  56.5 4.8 %products.12 = f32[2,144,512]{2,1,0:T(8,128)S(1)} custom-call(s32[3]{0:T(128)S(1)} %pad_add_fusion.place_ref._, f32[9216,1152]{1,0:T(8,128)} %rows_ref.19, f32[144,1152]{1,0:T(8,128)S(1)} %collective-permute-done.3.refs_0_.refs_1_), custom_call_target="tpu_custom_call" | custom-call | flops 1019215872 | bytes 4718592 | tf_op jit(solution)/shard_map/products/pallas_call | solution.py:101
  61.5 4.9 %products.18 = (f32[1,288,256]{2,1,0:T(8,128)S(1)}, f32[1,288,256]{2,1,0:T(8,128)S(1)}, f32[2,288,256]{2,1,0:T(8,128)S(1)}) custom-call(s32[3]{0:T(128)S(1)} %pad_add_fusion.place_ref._, f32[9216,1152]{1,0:T(8,128)} %rows_ref.19, f32[144,1152]{1,0:T(8,128)S(1)} %bitcast.25, f32[144,1152]{1,0:T(8,128)S(1)} %collective-permute-done.3.refs_0_.refs_1_, ...), custom_call_target="tpu_custom_call" | custom-call | flops 2038431744 | bytes 4718592 | tf_op jit(solution)/shard_map/products/pallas_call | solution.py:101
  66.8 4.8 %products.11 = (f32[1,144,512]{2,1,0:T(8,128)S(1)}, f32[1,144,512]{2,1,0:T(8,128)S(1)}) custom-call(s32[3]{0:T(128)S(1)} %pad_add_fusion.place_ref._, f32[9216,1152]{1,0:T(8,128)} %rows_ref.19, f32[144,1152]{1,0:T(8,128)S(1)} %bitcast.26, f32[2,144,512]{2,1,0:T(8,128)S(1)} %collective-permute-done.refs_1_), custom_call_target="tpu_custom_call" | custom-call | flops 1019215872 | bytes 4718592 | tf_op jit(solution)/shard_map/products/pallas_call | solution.py:101
  75.4 6.1 %collective-permute-done.1 = f32[1,144,512]{2,1,0:T(8,128)S(1)} collective-permute-done((f32[1,144,512]{2,1,0:T(8,128)S(1)}, f32[1,144,512]{2,1,0:T(8,128)S(1)}, u32[]{:S(2)}, u32[]{:S(2)}) %collective-permute-start.1) | collective-permute-done | bytes 294944 | tf_op jit(solution)/shard_map/ppermute | solution.py:195
  82.2 1.9 %collective-permute-start.2 = (f32[1,72,512]{2,1,0:T(8,128)S(1)}, f32[1,72,512]{2,1,0:T(8,128)S(1)}, u32[]{:S(2)}, u32[]{:S(2)}) collective-permute-start(f32[1,72,512]{2,1,0:T(8,128)S(1)} %get-tuple-element.52), channel_id=1, source_target_pairs={{0,4},{4,0},{8,12},{12,8},{1,5},{5,1},{9,13},{13,9},{2,6},{6,2},{1... | collective-permute-start | bytes 442376 | tf_op jit(solution)/shard_map/ppermute | solution.py:204
  84.0 4.8 %products.13 = (f32[1,144,512]{2,1,0:T(8,128)S(1)}, f32[1,144,512]{2,1,0:T(8,128)S(1)}) custom-call(s32[3]{0:T(128)S(1)} %pad_add_fusion.place_ref._, f32[9216,1152]{1,0:T(8,128)} %rows_ref.19, f32[144,1152]{1,0:T(8,128)S(1)} %collective-permute-done.3.refs_0_.refs_1_, f32[2,144,512]{2,1,0:T(8,128)S(1)} %collective-permute-done.4.refs_1_), custom_call_target="tpu_custom_call" | custom-call | flops 1019215872 | bytes 4718592 | tf_op jit(solution)/shard_map/products/pallas_call | solution.py:101
  92.4 3.5 %products.19 = (f32[1,288,256]{2,1,0:T(8,128)S(1)}, f32[1,288,256]{2,1,0:T(8,128)S(1)}) custom-call(s32[3]{0:T(128)S(1)} %pad_add_fusion.place_ref._, f32[9216,1152]{1,0:T(8,128)} %rows_ref.19, f32[144,1152]{1,0:T(8,128)S(1)} %bitcast.27, f32[144,1152]{1,0:T(8,128)S(1)} %collective-permute-done.3.refs_0_.refs_1_, ...), custom_call_target="tpu_custom_call" | custom-call | flops 1019215872 | bytes 2359296 | tf_op jit(solution)/shard_map/products/pallas_call | solution.py:101
  97.2 9.7 %collective-permute-done.13 = f32[1,288,512]{2,1,0:T(8,128)S(1)} collective-permute-done((f32[1,288,512]{2,1,0:T(8,128)S(1)}, f32[1,288,512]{2,1,0:T(8,128)S(1)}, u32[]{:S(2)}, u32[]{:S(2)}) %collective-permute-start.13) | collective-permute-done | bytes 589856 | tf_op jit(solution)/shard_map/ppermute | solution.py:195
  106.9 1.8 %collective-permute-start.10 = (f32[2,72,512]{2,1,0:T(8,128)S(1)}, f32[2,72,512]{2,1,0:T(8,128)S(1)}, u32[]{:S(2)}, u32[]{:S(2)}) collective-permute-start(f32[2,72,512]{2,1,0:T(8,128)S(1)} %get-tuple-element.62), channel_id=1, source_target_pairs={{0,4},{4,0},{8,12},{12,8},{1,5},{5,1},{9,13},{13,9},{2,6},{6,2},{1... | collective-permute-start | bytes 884744 | tf_op jit(solution)/shard_map/ppermute | solution.py:204
  109.3 3.9 %collective-permute-done.5 = f32[1,144,512]{2,1,0:T(8,128)S(1)} collective-permute-done((f32[1,144,512]{2,1,0:T(8,128)S(1)}, f32[1,144,512]{2,1,0:T(8,128)S(1)}, u32[]{:S(2)}, u32[]{:S(2)}) %collective-permute-start.5) | collective-permute-done | bytes 294944 | tf_op jit(solution)/shard_map/ppermute | solution.py:195
  113.2 1.8 %collective-permute-start.14 = (f32[2,72,512]{2,1,0:T(8,128)S(1)}, f32[2,72,512]{2,1,0:T(8,128)S(1)}, u32[]{:S(2)}, u32[]{:S(2)}) collective-permute-start(f32[2,72,512]{2,1,0:T(8,128)S(1)} %get-tuple-element.69), channel_id=1, source_target_pairs={{0,4},{4,0},{8,12},{12,8},{1,5},{5,1},{9,13},{13,9},{2,6},{6,2},{1... | collective-permute-start | bytes 884744 | tf_op jit(solution)/shard_map/ppermute | solution.py:204
  115.6 3.9 %collective-permute-done.17 = f32[1,288,256]{2,1,0:T(8,128)S(1)} collective-permute-done((f32[1,288,256]{2,1,0:T(8,128)S(1)}, f32[1,288,256]{2,1,0:T(8,128)S(1)}, u32[]{:S(2)}, u32[]{:S(2)}) %collective-permute-start.17) | collective-permute-done | bytes 294944 | tf_op jit(solution)/shard_map/ppermute | solution.py:195
  119.5 1.8 %collective-permute-start.6 = (f32[1,72,512]{2,1,0:T(8,128)S(1)}, f32[1,72,512]{2,1,0:T(8,128)S(1)}, u32[]{:S(2)}, u32[]{:S(2)}) collective-permute-start(f32[1,72,512]{2,1,0:T(8,128)S(1)} %get-tuple-element.56), channel_id=1, source_target_pairs={{0,4},{4,0},{8,12},{12,8},{1,5},{5,1},{9,13},{13,9},{2,6},{6,2},{1... | collective-permute-start | bytes 442376 | tf_op jit(solution)/shard_map/ppermute | solution.py:204
  121.9 3.9 %collective-permute-done.21 = f32[1,288,256]{2,1,0:T(8,128)S(1)} collective-permute-done((f32[1,288,256]{2,1,0:T(8,128)S(1)}, f32[1,288,256]{2,1,0:T(8,128)S(1)}, u32[]{:S(2)}, u32[]{:S(2)}) %collective-permute-start.21) | collective-permute-done | bytes 294944 | tf_op jit(solution)/shard_map/ppermute | solution.py:195
  125.8 1.8 %collective-permute-start.18 = (f32[2,72,256]{2,1,0:T(8,128)S(1)}, f32[2,72,256]{2,1,0:T(8,128)S(1)}, u32[]{:S(2)}, u32[]{:S(2)}) collective-permute-start(f32[2,72,256]{2,1,0:T(8,128)S(1)} %get-tuple-element.76), channel_id=1, source_target_pairs={{0,4},{4,0},{8,12},{12,8},{1,5},{5,1},{9,13},{13,9},{2,6},{6,2},{1... | collective-permute-start | bytes 442376 | tf_op jit(solution)/shard_map/ppermute | solution.py:204
  128.2 3.1 %collective-permute-done.25 = f32[1,288,256]{2,1,0:T(8,128)S(1)} collective-permute-done((f32[1,288,256]{2,1,0:T(8,128)S(1)}, f32[1,288,256]{2,1,0:T(8,128)S(1)}, u32[]{:S(2)}, u32[]{:S(2)}) %collective-permute-start.25) | collective-permute-done | bytes 294944 | tf_op jit(solution)/shard_map/ppermute | solution.py:195
  131.3 1.8 %collective-permute-start.22 = (f32[2,72,256]{2,1,0:T(8,128)S(1)}, f32[2,72,256]{2,1,0:T(8,128)S(1)}, u32[]{:S(2)}, u32[]{:S(2)}) collective-permute-start(f32[2,72,256]{2,1,0:T(8,128)S(1)} %get-tuple-element.83), channel_id=1, source_target_pairs={{0,4},{4,0},{8,12},{12,8},{1,5},{5,1},{9,13},{13,9},{2,6},{6,2},{1... | collective-permute-start | bytes 442376 | tf_op jit(solution)/shard_map/ppermute | solution.py:204
  134.6 2.9 %collective-permute-start.7 = (f32[72,512]{1,0:T(8,128)S(1)}, f32[72,512]{1,0:T(8,128)S(1)}, u32[]{:S(2)}, u32[]{:S(2)}) collective-permute-start(f32[72,512]{1,0:T(8,128)S(1)} %get-tuple-element.58), channel_id=1, source_target_pairs={{0,8},{4,12},{8,0},{12,4},{1,9},{5,13},{9,1},{13,5},{2,10},{6,14},... | collective-permute-start | bytes 442376 | tf_op jit(solution)/shard_map/ppermute | solution.py:208
  138.9 2.9 %collective-permute-start.15 = (f32[72,512]{1,0:T(8,128)S(1)}, f32[72,512]{1,0:T(8,128)S(1)}, u32[]{:S(2)}, u32[]{:S(2)}) collective-permute-start(f32[72,512]{1,0:T(8,128)S(1)} %get-tuple-element.71), channel_id=1, source_target_pairs={{0,8},{4,12},{8,0},{12,4},{1,9},{5,13},{9,1},{13,5},{2,10},{6,14},... | collective-permute-start | bytes 442376 | tf_op jit(solution)/shard_map/ppermute | solution.py:208
  144.1 1.9 %collective-permute-start.23 = (f32[72,256]{1,0:T(8,128)S(1)}, f32[72,256]{1,0:T(8,128)S(1)}, u32[]{:S(2)}, u32[]{:S(2)}) collective-permute-start(f32[72,256]{1,0:T(8,128)S(1)} %get-tuple-element.85), channel_id=1, source_target_pairs={{0,8},{4,12},{8,0},{12,4},{1,9},{5,13},{9,1},{13,5},{2,10},{6,14},... | collective-permute-start | bytes 221192 | tf_op jit(solution)/shard_map/ppermute | solution.py:208
  147.6 10.6 %collective-permute-done.11.refs_3_ = f32[72,512]{1,0:T(8,128)S(1)} collective-permute-done((f32[72,512]{1,0:T(8,128)S(1)}, f32[72,512]{1,0:T(8,128)S(1)}, u32[]{:S(2)}, u32[]{:S(2)}) %collective-permute-start.11) | collective-permute-done | bytes 147488 | tf_op jit(solution)/shard_map/ppermute | solution.py:208
  158.2 3.9 %collective-permute-done.15.refs_5_ = f32[72,512]{1,0:T(8,128)S(1)} collective-permute-done((f32[72,512]{1,0:T(8,128)S(1)}, f32[72,512]{1,0:T(8,128)S(1)}, u32[]{:S(2)}, u32[]{:S(2)}) %collective-permute-start.15) | collective-permute-done | bytes 147488 | tf_op jit(solution)/shard_map/ppermute | solution.py:208
  (53 shorter events, 26.5 us)
Async XLA Ops:
  0.0 18.1 %collective-permute-start.3 = (f32[144,1152]{1,0:T(8,128)}, f32[144,1152]{1,0:T(8,128)S(1)}, u32[]{:S(2)}, u32[]{:S(2)}) collective-permute-start(f32[144,1152]{1,0:T(8,128)} %bitcast.19), channel_id=1, source_target_pairs={{0,16},{16,0},{1,17},{17,1},{2,18},{18,2},{3,19},{19,3},{4,20},{20... | collective-permute-start | bytes 1990664 | tf_op jit(solution)/shard_map/ppermute | solution.py:174
  18.1 1.1 copy-start
  24.1 2.9 %collective-permute-start.8 = (f32[2,288,512]{2,1,0:T(8,128)S(1)}, f32[2,288,512]{2,1,0:T(8,128)S(1)}, u32[]{:S(2)}, u32[]{:S(2)}) collective-permute-start(f32[2,288,512]{2,1,0:T(8,128)S(1)} %products.14), channel_id=1, source_target_pairs={{0,1},{1,0},{2,3},{3,2},{4,5},{5,4},{6,7},{7,6},{8,9},{9,8},{10,11... | collective-permute-start | bytes 3538952 | tf_op jit(solution)/shard_map/ppermute | solution.py:198
  34.7 2.9 %collective-permute-start.12 = (f32[2,288,512]{2,1,0:T(8,128)S(1)}, f32[2,288,512]{2,1,0:T(8,128)S(1)}, u32[]{:S(2)}, u32[]{:S(2)}) collective-permute-start(f32[2,288,512]{2,1,0:T(8,128)S(1)} %get-tuple-element.65), channel_id=1, source_target_pairs={{0,1},{1,0},{2,3},{3,2},{4,5},{5,4},{6,7},{7,6},{8,9},{9,8},{10,11... | collective-permute-start | bytes 3538952 | tf_op jit(solution)/shard_map/ppermute | solution.py:198
  43.9 2.1 %collective-permute-start.16 = (f32[2,288,256]{2,1,0:T(8,128)S(1)}, f32[2,288,256]{2,1,0:T(8,128)S(1)}, u32[]{:S(2)}, u32[]{:S(2)}) collective-permute-start(f32[2,288,256]{2,1,0:T(8,128)S(1)} %get-tuple-element.72), channel_id=1, source_target_pairs={{0,1},{1,0},{2,3},{3,2},{4,5},{5,4},{6,7},{7,6},{8,9},{9,8},{10,11... | collective-permute-start | bytes 1769480 | tf_op jit(solution)/shard_map/ppermute | solution.py:198
  50.9 10.6 %collective-permute-start.20 = (f32[2,288,256]{2,1,0:T(8,128)S(1)}, f32[2,288,256]{2,1,0:T(8,128)S(1)}, u32[]{:S(2)}, u32[]{:S(2)}) collective-permute-start(f32[2,288,256]{2,1,0:T(8,128)S(1)} %get-tuple-element.79), channel_id=1, source_target_pairs={{0,1},{1,0},{2,3},{3,2},{4,5},{5,4},{6,7},{7,6},{8,9},{9,8},{10,11... | collective-permute-start | bytes 1769480 | tf_op jit(solution)/shard_map/ppermute | solution.py:198
  56.0 5.5 %copy-start.1 = (f32[1152,144]{0,1:T(8,128)S(1)}, f32[1152,144]{0,1:T(8,128)}, u32[]{:S(2)}) copy-start(f32[1152,144]{0,1:T(8,128)} %param.3) | copy-start | bytes 1990660
  56.1 10.8 %collective-permute-start = (f32[2,144,512]{2,1,0:T(8,128)S(1)}, f32[2,144,512]{2,1,0:T(8,128)S(1)}, u32[]{:S(2)}, u32[]{:S(2)}) collective-permute-start(f32[2,144,512]{2,1,0:T(8,128)S(1)} %products.10), channel_id=1, source_target_pairs={{0,1},{1,0},{2,3},{3,2},{4,5},{5,4},{6,7},{7,6},{8,9},{9,8},{10,11... | collective-permute-start | bytes 1769480 | tf_op jit(solution)/shard_map/ppermute | solution.py:198
  61.3 22.8 %collective-permute-start.4 = (f32[2,144,512]{2,1,0:T(8,128)S(1)}, f32[2,144,512]{2,1,0:T(8,128)S(1)}, u32[]{:S(2)}, u32[]{:S(2)}) collective-permute-start(f32[2,144,512]{2,1,0:T(8,128)S(1)} %products.12), channel_id=1, source_target_pairs={{0,1},{1,0},{2,3},{3,2},{4,5},{5,4},{6,7},{7,6},{8,9},{9,8},{10,11... | collective-permute-start | bytes 1769480 | tf_op jit(solution)/shard_map/ppermute | solution.py:198
  66.4 24.5 %collective-permute-start.24 = (f32[2,288,256]{2,1,0:T(8,128)S(1)}, f32[2,288,256]{2,1,0:T(8,128)S(1)}, u32[]{:S(2)}, u32[]{:S(2)}) collective-permute-start(f32[2,288,256]{2,1,0:T(8,128)S(1)} %get-tuple-element.86), channel_id=1, source_target_pairs={{0,1},{1,0},{2,3},{3,2},{4,5},{5,4},{6,7},{7,6},{8,9},{9,8},{10,11... | collective-permute-start | bytes 1769480 | tf_op jit(solution)/shard_map/ppermute | solution.py:198
  71.6 9.9 %collective-permute-start.1 = (f32[1,144,512]{2,1,0:T(8,128)S(1)}, f32[1,144,512]{2,1,0:T(8,128)S(1)}, u32[]{:S(2)}, u32[]{:S(2)}) collective-permute-start(f32[1,144,512]{2,1,0:T(8,128)S(1)} %get-tuple-element.50), channel_id=1, source_target_pairs={{0,2},{1,3},{2,0},{3,1},{4,6},{5,7},{6,4},{7,5},{8,10},{9,11},{10,... | collective-permute-start | bytes 884744 | tf_op jit(solution)/shard_map/ppermute | solution.py:195
  73.4 22.6 %collective-permute-start.9 = (f32[1,288,512]{2,1,0:T(8,128)S(1)}, f32[1,288,512]{2,1,0:T(8,128)S(1)}, u32[]{:S(2)}, u32[]{:S(2)}) collective-permute-start(f32[1,288,512]{2,1,0:T(8,128)S(1)} %get-tuple-element.60), channel_id=1, source_target_pairs={{0,2},{1,3},{2,0},{3,1},{4,6},{5,7},{6,4},{7,5},{8,10},{9,11},{10,... | collective-permute-start | bytes 1769480 | tf_op jit(solution)/shard_map/ppermute | solution.py:195
  73.7 33.1 %collective-permute-start.13 = (f32[1,288,512]{2,1,0:T(8,128)S(1)}, f32[1,288,512]{2,1,0:T(8,128)S(1)}, u32[]{:S(2)}, u32[]{:S(2)}) collective-permute-start(f32[1,288,512]{2,1,0:T(8,128)S(1)} %get-tuple-element.67), channel_id=1, source_target_pairs={{0,2},{1,3},{2,0},{3,1},{4,6},{5,7},{6,4},{7,5},{8,10},{9,11},{10,... | collective-permute-start | bytes 1769480 | tf_op jit(solution)/shard_map/ppermute | solution.py:195
  82.2 8.2 %collective-permute-start.2 = (f32[1,72,512]{2,1,0:T(8,128)S(1)}, f32[1,72,512]{2,1,0:T(8,128)S(1)}, u32[]{:S(2)}, u32[]{:S(2)}) collective-permute-start(f32[1,72,512]{2,1,0:T(8,128)S(1)} %get-tuple-element.52), channel_id=1, source_target_pairs={{0,4},{4,0},{8,12},{12,8},{1,5},{5,1},{9,13},{13,9},{2,6},{6,2},{1... | collective-permute-start | bytes 442376 | tf_op jit(solution)/shard_map/ppermute | solution.py:204
  88.8 24.3 %collective-permute-start.5 = (f32[1,144,512]{2,1,0:T(8,128)S(1)}, f32[1,144,512]{2,1,0:T(8,128)S(1)}, u32[]{:S(2)}, u32[]{:S(2)}) collective-permute-start(f32[1,144,512]{2,1,0:T(8,128)S(1)} %get-tuple-element.54), channel_id=1, source_target_pairs={{0,2},{1,3},{2,0},{3,1},{4,6},{5,7},{6,4},{7,5},{8,10},{9,11},{10,... | collective-permute-start | bytes 884744 | tf_op jit(solution)/shard_map/ppermute | solution.py:195
  90.4 29.1 %collective-permute-start.17 = (f32[1,288,256]{2,1,0:T(8,128)S(1)}, f32[1,288,256]{2,1,0:T(8,128)S(1)}, u32[]{:S(2)}, u32[]{:S(2)}) collective-permute-start(f32[1,288,256]{2,1,0:T(8,128)S(1)} %get-tuple-element.74), channel_id=1, source_target_pairs={{0,2},{1,3},{2,0},{3,1},{4,6},{5,7},{6,4},{7,5},{8,10},{9,11},{10,... | collective-permute-start | bytes 884744 | tf_op jit(solution)/shard_map/ppermute | solution.py:195
  90.9 34.9 %collective-permute-start.21 = (f32[1,288,256]{2,1,0:T(8,128)S(1)}, f32[1,288,256]{2,1,0:T(8,128)S(1)}, u32[]{:S(2)}, u32[]{:S(2)}) collective-permute-start(f32[1,288,256]{2,1,0:T(8,128)S(1)} %get-tuple-element.81), channel_id=1, source_target_pairs={{0,2},{1,3},{2,0},{3,1},{4,6},{5,7},{6,4},{7,5},{8,10},{9,11},{10,... | collective-permute-start | bytes 884744 | tf_op jit(solution)/shard_map/ppermute | solution.py:195
  96.0 35.4 %collective-permute-start.25 = (f32[1,288,256]{2,1,0:T(8,128)S(1)}, f32[1,288,256]{2,1,0:T(8,128)S(1)}, u32[]{:S(2)}, u32[]{:S(2)}) collective-permute-start(f32[1,288,256]{2,1,0:T(8,128)S(1)} %get-tuple-element.88), channel_id=1, source_target_pairs={{0,2},{1,3},{2,0},{3,1},{4,6},{5,7},{6,4},{7,5},{8,10},{9,11},{10,... | collective-permute-start | bytes 884744 | tf_op jit(solution)/shard_map/ppermute | solution.py:195
  106.9 27.7 %collective-permute-start.10 = (f32[2,72,512]{2,1,0:T(8,128)S(1)}, f32[2,72,512]{2,1,0:T(8,128)S(1)}, u32[]{:S(2)}, u32[]{:S(2)}) collective-permute-start(f32[2,72,512]{2,1,0:T(8,128)S(1)} %get-tuple-element.62), channel_id=1, source_target_pairs={{0,4},{4,0},{8,12},{12,8},{1,5},{5,1},{9,13},{13,9},{2,6},{6,2},{1... | collective-permute-start | bytes 884744 | tf_op jit(solution)/shard_map/ppermute | solution.py:204
  113.2 24.9 %collective-permute-start.14 = (f32[2,72,512]{2,1,0:T(8,128)S(1)}, f32[2,72,512]{2,1,0:T(8,128)S(1)}, u32[]{:S(2)}, u32[]{:S(2)}) collective-permute-start(f32[2,72,512]{2,1,0:T(8,128)S(1)} %get-tuple-element.69), channel_id=1, source_target_pairs={{0,4},{4,0},{8,12},{12,8},{1,5},{5,1},{9,13},{13,9},{2,6},{6,2},{1... | collective-permute-start | bytes 884744 | tf_op jit(solution)/shard_map/ppermute | solution.py:204
  119.5 14.2 %collective-permute-start.6 = (f32[1,72,512]{2,1,0:T(8,128)S(1)}, f32[1,72,512]{2,1,0:T(8,128)S(1)}, u32[]{:S(2)}, u32[]{:S(2)}) collective-permute-start(f32[1,72,512]{2,1,0:T(8,128)S(1)} %get-tuple-element.56), channel_id=1, source_target_pairs={{0,4},{4,0},{8,12},{12,8},{1,5},{5,1},{9,13},{13,9},{2,6},{6,2},{1... | collective-permute-start | bytes 442376 | tf_op jit(solution)/shard_map/ppermute | solution.py:204
  125.8 13.0 %collective-permute-start.18 = (f32[2,72,256]{2,1,0:T(8,128)S(1)}, f32[2,72,256]{2,1,0:T(8,128)S(1)}, u32[]{:S(2)}, u32[]{:S(2)}) collective-permute-start(f32[2,72,256]{2,1,0:T(8,128)S(1)} %get-tuple-element.76), channel_id=1, source_target_pairs={{0,4},{4,0},{8,12},{12,8},{1,5},{5,1},{9,13},{13,9},{2,6},{6,2},{1... | collective-permute-start | bytes 442376 | tf_op jit(solution)/shard_map/ppermute | solution.py:204
  131.3 11.0 %collective-permute-start.22 = (f32[2,72,256]{2,1,0:T(8,128)S(1)}, f32[2,72,256]{2,1,0:T(8,128)S(1)}, u32[]{:S(2)}, u32[]{:S(2)}) collective-permute-start(f32[2,72,256]{2,1,0:T(8,128)S(1)} %get-tuple-element.83), channel_id=1, source_target_pairs={{0,4},{4,0},{8,12},{12,8},{1,5},{5,1},{9,13},{13,9},{2,6},{6,2},{1... | collective-permute-start | bytes 442376 | tf_op jit(solution)/shard_map/ppermute | solution.py:204
  133.7 10.3 %collective-permute-start.26 = (f32[2,72,256]{2,1,0:T(8,128)S(1)}, f32[2,72,256]{2,1,0:T(8,128)S(1)}, u32[]{:S(2)}, u32[]{:S(2)}) collective-permute-start(f32[2,72,256]{2,1,0:T(8,128)S(1)} %get-tuple-element.90), channel_id=1, source_target_pairs={{0,4},{4,0},{8,12},{12,8},{1,5},{5,1},{9,13},{13,9},{2,6},{6,2},{1... | collective-permute-start | bytes 442376 | tf_op jit(solution)/shard_map/ppermute | solution.py:204
  134.6 11.9 %collective-permute-start.7 = (f32[72,512]{1,0:T(8,128)S(1)}, f32[72,512]{1,0:T(8,128)S(1)}, u32[]{:S(2)}, u32[]{:S(2)}) collective-permute-start(f32[72,512]{1,0:T(8,128)S(1)} %get-tuple-element.58), channel_id=1, source_target_pairs={{0,8},{4,12},{8,0},{12,4},{1,9},{5,13},{9,1},{13,5},{2,10},{6,14},... | collective-permute-start | bytes 442376 | tf_op jit(solution)/shard_map/ppermute | solution.py:208
  138.1 20.1 %collective-permute-start.11 = (f32[72,512]{1,0:T(8,128)S(1)}, f32[72,512]{1,0:T(8,128)S(1)}, u32[]{:S(2)}, u32[]{:S(2)}) collective-permute-start(f32[72,512]{1,0:T(8,128)S(1)} %get-tuple-element.64), channel_id=1, source_target_pairs={{0,8},{4,12},{8,0},{12,4},{1,9},{5,13},{9,1},{13,5},{2,10},{6,14},... | collective-permute-start | bytes 442376 | tf_op jit(solution)/shard_map/ppermute | solution.py:208
  138.9 23.3 %collective-permute-start.15 = (f32[72,512]{1,0:T(8,128)S(1)}, f32[72,512]{1,0:T(8,128)S(1)}, u32[]{:S(2)}, u32[]{:S(2)}) collective-permute-start(f32[72,512]{1,0:T(8,128)S(1)} %get-tuple-element.71), channel_id=1, source_target_pairs={{0,8},{4,12},{8,0},{12,4},{1,9},{5,13},{9,1},{13,5},{2,10},{6,14},... | collective-permute-start | bytes 442376 | tf_op jit(solution)/shard_map/ppermute | solution.py:208
  142.3 21.4 %collective-permute-start.19 = (f32[72,256]{1,0:T(8,128)S(1)}, f32[72,256]{1,0:T(8,128)S(1)}, u32[]{:S(2)}, u32[]{:S(2)}) collective-permute-start(f32[72,256]{1,0:T(8,128)S(1)} %get-tuple-element.78), channel_id=1, source_target_pairs={{0,8},{4,12},{8,0},{12,4},{1,9},{5,13},{9,1},{13,5},{2,10},{6,14},... | collective-permute-start | bytes 221192 | tf_op jit(solution)/shard_map/ppermute | solution.py:208
  144.1 21.1 %collective-permute-start.23 = (f32[72,256]{1,0:T(8,128)S(1)}, f32[72,256]{1,0:T(8,128)S(1)}, u32[]{:S(2)}, u32[]{:S(2)}) collective-permute-start(f32[72,256]{1,0:T(8,128)S(1)} %get-tuple-element.85), channel_id=1, source_target_pairs={{0,8},{4,12},{8,0},{12,4},{1,9},{5,13},{9,1},{13,5},{2,10},{6,14},... | collective-permute-start | bytes 221192 | tf_op jit(solution)/shard_map/ppermute | solution.py:208
  146.5 19.5 %collective-permute-start.27 = (f32[72,256]{1,0:T(8,128)S(1)}, f32[72,256]{1,0:T(8,128)S(1)}, u32[]{:S(2)}, u32[]{:S(2)}) collective-permute-start(f32[72,256]{1,0:T(8,128)S(1)} %get-tuple-element.92), channel_id=1, source_target_pairs={{0,8},{4,12},{8,0},{12,4},{1,9},{5,13},{9,1},{13,5},{2,10},{6,14},... | collective-permute-start | bytes 221192 | tf_op jit(solution)/shard_map/ppermute | solution.py:208
